TPU v7x, 32 devices: a whole 2x2x4 slice. The times are simulated.
32 devices in a mesh: region: 4 (over x, core), sector: 8 (over z, y).
Axes of the slice: x: 2, y: 2, z: 4, core: 2. Of those that a mesh axis runs over, the one named last changes fastest.
Arguments:
- env_left: bfloat16 [4, 8, 2048, 2048], P('region', None, 'sector'), may hold values from -6 to 6
- site_tensor: bfloat16 [4, 2048, 2, 2048], P('region', 'sector'), may hold values from -0.125 to 0.125
- mpo_tensor: float32 [4, 8, 8, 2, 2], P('region'), may hold values from -1 to 1
- env_right: bfloat16 [4, 8, 2048, 2048], P('region', None, 'sector'), may hold values from -0.046875 to 0.046875
- bond_tensor: bfloat16 [4, 2048, 2048], P('region'), may hold values from -0.125 to 0.125
Outputs:
- env_next: bfloat16 [4, 8, 2048, 2048], P('region', None, 'sector')
- bond_image: bfloat16 [4, 2048, 2048], P('region', 'sector')
All inputs are finite; a program needn't handle non-finite values.
Results may differ from a plain program's by a relative error of at most 0.0065.
Values may be sent and summed in bfloat16 or wider, within the bound.
A program may use at most 192 MiB of HBM per device.

v0:
```python
import jax
import jax.numpy as jnp
from jax import lax
from jax.sharding import PartitionSpec as P


def shifted(block, axis, distance):
    devices = range(lax.axis_size(axis))
    route = [((i - distance) % len(devices), i) for i in devices]
    return lax.ppermute(block, axis, route)


def bond_side(env_right, bond_tensor):
    right_next = shifted(env_right, "region", -1)[0]
    return jnp.einsum(
        "wbc,kc->wbk", right_next, bond_tensor[0], preferred_element_type=jnp.float32
    ).astype(jnp.bfloat16)


def absorb_side(env_left, site_tensor, mpo_tensor):
    gathered = lax.all_gather(site_tensor, "sector", axis=1, tiled=True)[0]
    half_done = jnp.einsum(
        "wak,ksc->wasc", env_left[0], gathered, preferred_element_type=jnp.float32
    )
    carried = jnp.einsum(
        "vwst,vatc->wsac", mpo_tensor[0], half_done, precision=lax.Precision.HIGHEST
    ).astype(jnp.bfloat16)
    width_mpo, states, row_total, columns = carried.shape
    return (gathered, carried.reshape(width_mpo * states, row_total, columns))


def local(env_left, site_tensor, mpo_tensor, env_right, bond_tensor):
    width_mpo = env_left.shape[1]
    states = site_tensor.shape[2]
    gathered, carried = absorb_side(env_left, site_tensor, mpo_tensor)
    bond_right = bond_side(env_right, bond_tensor)
    carried_moved = lax.all_to_all(carried, "sector", split_axis=2, concat_axis=1, tiled=True)
    bond_moved = lax.all_to_all(bond_right, "sector", split_axis=2, concat_axis=1, tiled=True)
    full_rows = carried_moved.shape[1]
    local_cols = carried_moved.shape[2]
    carried_moved = carried_moved.reshape(width_mpo, states, full_rows, local_cols)
    env_new = jnp.einsum(
        "wsac,asb->wcb", carried_moved, gathered, preferred_element_type=jnp.float32
    ).astype(jnp.bfloat16)
    image_rows = lax.psum_scatter(
        jnp.einsum("wka,wbk->ab", env_new, bond_moved, preferred_element_type=jnp.float32),
        "sector",
        scatter_dimension=0,
        tiled=True,
    )
    return (env_new[None], image_rows.astype(jnp.bfloat16)[None])


def solution(mesh):
    return jax.shard_map(
        local,
        mesh=mesh,
        in_specs=(
            P("region", None, "sector", None),
            P("region", "sector", None, None),
            P("region", None, None, None, None),
            P("region", None, "sector", None),
            P("region", None, None),
        ),
        out_specs=(P("region", None, "sector", None), P("region", "sector", None)),
        check_vma=False,
    )
```

profile of v0, /device:TPU:0, one launch (start us, length us, event | category | flops | bytes accessed | tf_op | source)
XLA Modules:
  0.0 1278.0 jit_solution(12516192060234852822)
XLA Ops:
  7.2 0.0 all-gather.2.cloned.1.call-start
  7.2 3.8 copy.18
  11.0 0.0 all-gather.2.cloned.1.call-update
  11.1 2.5 collective-permute-start
  13.5 1.4 copy.20
  14.9 89.9 %collective-permute-done = bf16[1,8,256,2048]{3,2,1,0:T(8,128)(2,1)} collective-permute-done((bf16[1,8,256,2048]{3,2,1,0:T(8,128)(2,1)}, bf16[1,8,256,2048]{3,2,1,0:T(8,128)(2,1)}, u32[]{:S(2)}, u32[]{:S(2)}) %collective-permute-start) | collective-permute-done | bytes 8388640 | tf_op jit(solution)/shard_map/ppermute | solution.py:10
  104.8 23.7 %fusion.15 = bf16[8,256,2048]{2,1,0:T(8,128)(2,1)} fusion(bf16[1,2048,2048]{2,1,0:T(8,128)(2,1)} %param.9, bf16[1,8,256,2048]{3,2,1,0:T(8,128)(2,1)} %collective-permute-done), kind=kOutput, calls=%fused_computation.14 | convolution fusion | flops 17184063488 | bytes 25165824 | tf_op jit(solution)/shard_map/wbc,kc->wbk/dot_general | solution.py:15
  128.5 12.6 copy.25
  141.1 6.4 all-to-all-start.1
  147.6 232.6 %all-gather.2.cloned.1.call-done = bf16[1,2048,2,2048]{3,1,2,0:T(8,128)(2,1)} async-done(((bf16[1,256,2,2048]{3,1,2,0:T(8,128)(2,1)}), bf16[1,2048,2,2048]{3,1,2,0:T(8,128)(2,1)}) %all-gather.2.cloned.1.call-update) | async-done | bytes 16777232 | tf_op jit(solution)/shard_map/all_gather | solution.py:21
  380.2 0.0 copy-start
  380.2 50.8 %fusion.6 = f32[8,256,2,2048]{3,0,2,1:T(8,128)} fusion(bf16[1,2048,2,2048]{3,1,2,0:T(8,128)(2,1)} %all-gather.2.cloned.1.call-done, bf16[8,256,2048,1]{2,1,0,3:T(8,128)(2,1)} %bitcast.68), kind=kOutput, calls=%fused_computation.6 | convolution fusion | flops 34359738368 | bytes 58720256 | tf_op jit(solution)/shard_map/wak,ksc->wasc/dot_general | solution.py:22
  431.0 0.0 copy-done
  431.0 32.6 %fusion.8 = bf16[8,2,256,2048]{3,0,1,2:T(8,128)(2,1)S(1)} fusion(f32[8,256,2,2048]{3,0,2,1:T(8,128)} %fusion.6, f32[8,8,2,2]{0,1,3,2:T(8,128)S(1)} %copy-done), kind=kOutput, calls=%fused_computation.8 | convolution fusion | flops 1619001344 | bytes 50332672 | tf_op jit(solution)/shard_map/vwst,vatc->wsac/dot_general | solution.py:25
  463.6 20.9 %copy.21 = bf16[8,2,256,2048]{3,2,1,0:T(8,128)(2,1)} copy(bf16[8,2,256,2048]{3,0,1,2:T(8,128)(2,1)S(1)} %fusion.8) | data formatting | bytes 33554432 | tf_op jit(solution)/shard_map/convert_element_type | solution.py:27
  484.5 23.8 %copy.22 = bf16[16,256,2048]{1,0,2:T(8,128)(2,1)} copy(bf16[16,256,2048]{2,1,0:T(8,128)(2,1)} %bitcast.65) | data formatting | bytes 33554432 | tf_op jit(solution)/shard_map/reshape | solution.py:29
  508.3 0.0 all-to-all-done.1
  508.3 5.7 all-to-all-start
  514.0 0.0 reduce-scatter.2.cloned.1.call-start
  514.1 12.7 copy.26
  526.7 350.6 %all-to-all-done = bf16[16,256,2048]{1,0,2:T(8,128)(2,1)} async-done(((bf16[16,256,2048]{1,0,2:T(8,128)(2,1)}), bf16[16,256,2048]{1,0,2:T(8,128)(2,1)}, u32[]{:S(2)}, u32[]{:S(2)}) %all-to-all-start) | async-done | bytes 16777248 | tf_op jit(solution)/shard_map/all_to_all | solution.py:37
  877.3 18.1 %copy.24 = bf16[16,8,256,256]{2,1,3,0:T(8,128)(2,1)} copy(bf16[16,8,256,256]{2,0,3,1:T(8,128)(2,1)} %bitcast.14) | data formatting | bytes 33554432 | tf_op jit(solution)/shard_map/all_to_all | solution.py:37
  895.4 25.6 %reshape.12 = bf16[8,2,2048,256]{2,3,1,0:T(8,128)(2,1)} reshape(bf16[16,8,256,256]{2,1,3,0:T(8,128)(2,1)} %copy.24) | data formatting | bytes 33554432 | tf_op jit(solution)/shard_map/reshape | solution.py:41
  921.0 41.1 %bitcast_convert_fusion.1 = bf16[8,256,2048]{2,1,0:T(8,128)(2,1)S(1)} fusion(bf16[8,2,2048,256]{2,3,1,0:T(8,128)(2,1)} %reshape.12, bf16[1,2048,2,2048]{3,1,2,0:T(8,128)(2,1)} %all-gather.2.cloned.1.call-done), kind=kOutput, calls=%fused_computation.3 | convolution fusion | flops 34363932672 | bytes 41943040 | tf_op jit(solution)/shard_map/wsac,asb->wcb/dot_general | solution.py:42
  962.1 0.0 copy-start.1
  962.1 3.4 copy-done.1
  965.5 23.3 %convolution_bitcast_fusion = f32[2048,2048]{1,0:T(8,128)} fusion(bf16[8,256,2048]{2,1,0:T(8,128)(2,1)S(1)} %bitcast_convert_fusion.1, bf16[8,2048,256]{2,1,0:T(8,128)(2,1)} %bitcast.66), kind=kOutput, calls=%fused_computation.9 | convolution fusion | flops 17179869184 | bytes 33554432 | tf_op jit(solution)/shard_map/wka,wbk->ab/dot_general | solution.py:46
  988.8 0.0 reduce-scatter.2.cloned.1.call-update
  988.8 279.3 %reduce-scatter.2.cloned.1.call-done = f32[256,2048]{1,0:T(8,128)} async-done(((f32[2048,2048]{1,0:T(8,128)}), f32[256,2048]{1,0:T(8,128)}) %reduce-scatter.2.cloned.1.call-update) | async-done | bytes 2097168 | tf_op jit(solution)/shard_map/reduce_scatter | solution.py:45
  1268.2 2.7 convert_bitcast_fusion
Async XLA Ops:
  7.2 373.0 %all-gather.2.cloned.1.call-start = ((), (), s32[]{:S(2)}) async-start(), calls=%async_computation.3 | async-start | bytes 18874368 | tf_op jit(solution)/shard_map/all_gather | solution.py:21
  11.1 93.7 %collective-permute-start = (bf16[1,8,256,2048]{3,2,1,0:T(8,128)(2,1)}, bf16[1,8,256,2048]{3,2,1,0:T(8,128)(2,1)}, u32[]{:S(2)}, u32[]{:S(2)}) collective-permute-start(bf16[1,8,256,2048]{3,2,1,0:T(8,128)(2,1)} %param.8), channel_id=1, source_target_pairs={{8,0},{16,8},{24,16},{0,24},{9,1},{17,9},{25,17},{1,25},{10,2},{18... | collective-permute-start | bytes 25165832 | tf_op jit(solution)/shard_map/ppermute | solution.py:10
  141.1 367.2 %all-to-all-start.1 = ((bf16[8,256,2048]{1,0,2:T(8,128)(2,1)}), bf16[8,256,2048]{1,0,2:T(8,128)(2,1)}, u32[]{:S(2)}, u32[]{:S(2)}) async-start(bf16[8,256,2048]{1,0,2:T(8,128)(2,1)} %copy.25), calls=%async_computation.1 | async-start | bytes 16777216 | tf_op jit(solution)/shard_map/all_to_all | solution.py:38
  380.2 50.8 %copy-start = (f32[8,8,2,2]{0,1,3,2:T(8,128)S(1)}, f32[8,8,2,2]{0,1,3,2:T(8,128)}, u32[]{:S(2)}) copy-start(f32[8,8,2,2]{0,1,3,2:T(8,128)} %copy.20) | copy-start | bytes 3076
  508.3 369.0 %all-to-all-start = ((bf16[16,256,2048]{1,0,2:T(8,128)(2,1)}), bf16[16,256,2048]{1,0,2:T(8,128)(2,1)}, u32[]{:S(2)}, u32[]{:S(2)}) async-start(bf16[16,256,2048]{1,0,2:T(8,128)(2,1)} %copy.22), calls=%async_computation | async-start | bytes 33554432 | tf_op jit(solution)/shard_map/all_to_all | solution.py:37
  514.0 754.1 %reduce-scatter.2.cloned.1.call-start = ((), (), s32[]{:S(2)}) async-start(), calls=%async_computation.4 | async-start | bytes 18874368 | tf_op jit(solution)/shard_map/reduce_scatter | solution.py:45
  962.1 3.4 copy-start.1
Sparse Core Ops, SparseCore 0:
  11.2 368.9 all-gather.1
  988.9 279.1 reduce-scatter.1
where the time goes:
time: 1290 us; the launch traced here: 1280 us
  waiting for transfers between devices  952 us (74%)
  matrix products  171 us (13%)
  local copies, waits for them, and re-layouts  122 us (9%)
  starting transfers between devices  14.7 us (1%)
  between operations  14.4 us (1%)
    all_to_all x1, waiting for transfers between devices, local(): lax.all_to_all(carried, 'sector', split_axis=2, concat_axis=1, tiled=True)  351 us
    reduce_scatter x1, waiting for transfers between devices, local(): lax.psum_scatter(jnp.einsum('wka,wbk->ab', env_new, bond_moved, preferred...  279 us
    all_gather x1, waiting for transfers between devices, absorb_side(): gathered = lax.all_gather(site_tensor, 'sector', axis=1, tiled=True)[0]  233 us
    ppermute x1, waiting for transfers between devices, shifted(): return lax.ppermute(block, axis, route)  89.9 us
    dot_general x1, matrix products, absorb_side(): jnp.einsum('wak,ksc->wasc', env_left[0], gathered, preferred_element_type...  50.8 us
    dot_general x1, matrix products, local(): jnp.einsum('wsac,asb->wcb', carried_moved, gathered, preferred_element_ty...  41.1 us
    dot_general x1, matrix products, absorb_side(): jnp.einsum('vwst,vatc->wsac', mpo_tensor[0], half_done, precision=lax.Pre...  32.6 us
  transfers between devices with their start and end apart: 5, of which 4 were waited for; matrix products, arithmetic and copies ran while one was open for 14% of the time, Pallas kernels for 0%

commit v1 on v0

v1 whole, which is shorter than its diff:
```python
import functools

import jax
import jax.numpy as jnp
from jax import lax
from jax.experimental import pallas as pl
from jax.experimental.pallas import tpu as pltpu
from jax.sharding import PartitionSpec as P


GROUP = 16
LANES = 128
CHUNKS = 2
VMEM_LIMIT = 60 * 1024 * 1024


def shifted(block, axis, distance):
    devices = range(lax.axis_size(axis))
    route = [((i - distance) % len(devices), i) for i in devices]
    return lax.ppermute(block, axis, route)


def swap(blocks):
    return lax.all_to_all(blocks, "sector", split_axis=0, concat_axis=0, tiled=True)


def carried_kernel(mix_ref, env_ref, site_ref, *out_refs):
    width, rows, bond = env_ref.shape
    _, states, _, columns = site_ref.shape
    mix = mix_ref[...]
    mix_high = mix.astype(jnp.bfloat16)
    mix_low = (mix - mix_high.astype(jnp.float32)).astype(jnp.bfloat16)
    env = env_ref[...].reshape(width * rows, bond)
    half_done = [
        jnp.dot(env, site_ref[:, t].reshape(bond, columns), preferred_element_type=jnp.float32)
        .reshape(width, rows, columns)
        for t in range(states)
    ]
    dot = functools.partial(jnp.dot, preferred_element_type=jnp.float32)
    for g in range(rows // GROUP):
        span = slice(g * GROUP, (g + 1) * GROUP)
        x = jnp.concatenate(
            [h[:, span].reshape(width * GROUP, columns) for h in half_done], axis=0
        )
        high = x.astype(jnp.bfloat16)
        low = (x - high.astype(jnp.float32)).astype(jnp.bfloat16)
        y = dot(mix_high, high) + dot(mix_high, low) + dot(mix_low, high)
        y = y.astype(jnp.bfloat16).reshape(width, states, GROUP, columns)
        step = width // len(out_refs)
        for i, out_ref in enumerate(out_refs):
            out_ref[0, :, :, span, :] = y[i * step : (i + 1) * step]


def carried_blocks(env_left, gathered, mpo, row_tile):
    width, rows, bond = env_left.shape
    parts, states, depth, _ = gathered.shape
    columns = bond // parts
    eye = jnp.eye(GROUP, dtype=jnp.float32)
    side = width * states * GROUP
    mix = jnp.einsum("vwst,ij->wsitvj", mpo, eye, precision=lax.Precision.HIGHEST).reshape(side, side)
    step = width // CHUNKS
    out = jax.ShapeDtypeStruct((parts, step, states, rows, columns), jnp.bfloat16)
    return pl.pallas_call(
        carried_kernel,
        grid=(rows // row_tile, parts),
        in_specs=[
            pl.BlockSpec((side, side), lambda i, j: (0, 0)),
            pl.BlockSpec((width, row_tile, bond), lambda i, j: (0, i, 0)),
            pl.BlockSpec((parts, states, depth, columns), lambda i, j: (0, 0, 0, j)),
        ],
        out_specs=[
            pl.BlockSpec((1, step, states, row_tile, columns), lambda i, j: (j, 0, 0, i, 0))
        ] * CHUNKS,
        out_shape=[out] * CHUNKS,
        compiler_params=pltpu.CompilerParams(vmem_limit_bytes=VMEM_LIMIT),
        cost_estimate=pl.CostEstimate(
            flops=2 * width * rows * bond * bond * states,
            bytes_accessed=96 * 1024 * 1024,
            transcendentals=0,
        ),
    )(mix, env_left, gathered)


def env_kernel(x_ref, site_ref, *rest):
    out_ref, turned = rest[-2:]
    parts, count, states, depth, columns = x_ref.shape

    @pl.when(pl.program_id(0) == 0)
    def _():
        for n in range(parts):
            for s in range(states):
                at = (n * states + s) * depth
                for v in range(count):
                    turned[v * columns : (v + 1) * columns, at : at + depth] = x_ref[n, v, s].T

    site = site_ref[...].reshape(parts * states * depth, site_ref.shape[-1])
    total = jnp.dot(turned[...], site, preferred_element_type=jnp.float32)
    out_ref[...] = total.astype(jnp.bfloat16).reshape(out_ref.shape)


def env_chunk(moved, gathered, previous, chunk, width, tile):
    parts, count, states, depth, columns = moved.shape
    bond = gathered.shape[-1]
    operands = (moved, gathered) + (() if previous is None else (previous,))
    specs = [
        pl.BlockSpec(moved.shape, lambda j: (0, 0, 0, 0, 0), pipeline_mode=pl.Buffered(1)),
        pl.BlockSpec((parts, states, depth, tile), lambda j: (0, 0, 0, j)),
    ]
    if previous is not None:
        specs.append(pl.BlockSpec(memory_space=pl.ANY))
    return pl.pallas_call(
        env_kernel,
        grid=(bond // tile,),
        in_specs=specs,
        out_specs=pl.BlockSpec((count, columns, tile), lambda j: (chunk, 0, j)),
        out_shape=jax.ShapeDtypeStruct((width, columns, bond), jnp.bfloat16),
        scratch_shapes=[pltpu.VMEM((count * columns, parts * states * depth), jnp.bfloat16)],
        input_output_aliases={} if previous is None else {2: 0},
        compiler_params=pltpu.CompilerParams(vmem_limit_bytes=VMEM_LIMIT),
        cost_estimate=pl.CostEstimate(
            flops=2 * count * columns * parts * states * depth * bond,
            bytes_accessed=32 * 1024 * 1024,
            transcendentals=0,
        ),
    )(*operands)


def local(env_left, site_tensor, mpo_tensor, env_right, bond_tensor):
    parts = lax.axis_size("sector")
    width, rows, bond = env_left.shape[1:]
    columns = bond // parts
    gathered = lax.all_gather(site_tensor[0].transpose(1, 0, 2), "sector", axis=0)
    right_next = shifted(env_right, "region", -1)[0]
    bond_blocks = jnp.einsum(
        "dkc,wbc->dwkb",
        bond_tensor[0].reshape(parts, columns, bond),
        right_next,
        preferred_element_type=jnp.float32,
    ).astype(jnp.bfloat16)
    bond_blocks, gathered = lax.optimization_barrier((bond_blocks, gathered))
    bond_moved = swap(bond_blocks)
    carried = carried_blocks(env_left[0], gathered, mpo_tensor[0], min(rows, LANES))
    moved = []
    for i in range(CHUNKS):
        moved.append(swap(carried[i]))
    env_new = None
    for i in range(CHUNKS):
        env_new = env_chunk(moved[i], gathered, env_new, i, width, 2 * LANES)
    image = jnp.einsum(
        "wka,nwkb->anb", env_new, bond_moved, preferred_element_type=jnp.float32
    ).astype(jnp.bfloat16).reshape(bond, bond)
    image_rows = lax.psum_scatter(image, "sector", scatter_dimension=0, tiled=True)
    return (env_new[None], image_rows[None])


def plain_local(env_left, site_tensor, mpo_tensor, env_right, bond_tensor):
    width = env_left.shape[1]
    states = site_tensor.shape[2]
    gathered = lax.all_gather(site_tensor, "sector", axis=1, tiled=True)[0]
    half_done = jnp.einsum(
        "wak,ksc->wasc", env_left[0], gathered, preferred_element_type=jnp.float32
    )
    carried = jnp.einsum(
        "vwst,vatc->wsac", mpo_tensor[0], half_done, precision=lax.Precision.HIGHEST
    ).astype(jnp.bfloat16)
    carried = carried.reshape((width * states,) + carried.shape[2:])
    right_next = shifted(env_right, "region", -1)[0]
    bond_right = jnp.einsum(
        "wbc,kc->wbk", right_next, bond_tensor[0], preferred_element_type=jnp.float32
    ).astype(jnp.bfloat16)
    carried_moved = lax.all_to_all(carried, "sector", split_axis=2, concat_axis=1, tiled=True)
    bond_moved = lax.all_to_all(bond_right, "sector", split_axis=2, concat_axis=1, tiled=True)
    carried_moved = carried_moved.reshape((width, states) + carried_moved.shape[1:])
    env_new = jnp.einsum(
        "wsac,asb->wcb", carried_moved, gathered, preferred_element_type=jnp.float32
    ).astype(jnp.bfloat16)
    image_rows = lax.psum_scatter(
        jnp.einsum("wka,wbk->ab", env_new, bond_moved, preferred_element_type=jnp.float32),
        "sector",
        scatter_dimension=0,
        tiled=True,
    )
    return (env_new[None], image_rows.astype(jnp.bfloat16)[None])


def solution(mesh):
    def body(env_left, site_tensor, mpo_tensor, env_right, bond_tensor):
        width, rows, bond = env_left.shape[1:]
        columns = bond // mesh.shape["sector"]
        tiled = rows % LANES == 0 and columns % LANES == 0 and width % CHUNKS == 0
        step = local if tiled else plain_local
        return step(env_left, site_tensor, mpo_tensor, env_right, bond_tensor)

    return jax.shard_map(
        body,
        mesh=mesh,
        in_specs=(
            P("region", None, "sector", None),
            P("region", "sector", None, None),
            P("region", None, None, None, None),
            P("region", None, "sector", None),
            P("region", None, None),
        ),
        out_specs=(P("region", None, "sector", None), P("region", "sector", None)),
        check_vma=False,
    )
```

time: 1290 us -> 1050 us (0.81)
  waiting for transfers between devices: 952 us -> 653 us
  blocking collectives: 0 us -> 189 us
  matrix products: 171 us -> 47.3 us
  Pallas kernels: 0 us -> 109 us
  local copies, waits for them, and re-layouts: 122 us -> 26.1 us
    all_to_all x0 -> x1, blocking collectives: none -> 189 us  [swap(): lax.all_to_all(blocks, 'sector', split_axis=0, concat_axis=0, tiled=True)]
    reduce_scatter x1, waiting for transfers between devices: 279 us -> 147 us  [local(): lax.psum_scatter(image, 'sector', scatter_dimension=0, tiled=True)]
    dot_general x5 -> x2, matrix products: 171 us -> 47.3 us  [the longest x1 23.8 us: local(): jnp.einsum('dkc,wbc->dwkb', bond_tensor[0].reshape(parts, columns, bond),...]
    all_gather x1, waiting for transfers between devices: 233 us -> 113 us  [local(): lax.all_gather(site_tensor[0].transpose(1, 0, 2), 'sector', axis=0)]
    pallas_call x0 -> x3, Pallas kernels: none -> 109 us  [the longest x1 57 us: carried_blocks(): pl.pallas_call(carried_kernel, grid=(rows // row_tile, parts), in_specs=[...]
    all_to_all x2, waiting for transfers between devices: 351 us -> 304 us  [swap(): lax.all_to_all(blocks, 'sector', split_axis=0, concat_axis=0, tiled=True)]
    reshape x2, local copies, waits for them, and re-layouts: 49.4 us -> 13.9 us  [the longest x1 12.4 us: local(): image = jnp.einsum('wka,nwkb->anb', env_new, bond_moved, preferred_elemen...]
    convert_element_type x2 -> x0, local copies, waits for them, and re-layouts: 33.5 us -> none  [the longest x1 20.9 us: absorb_side(): carried = jnp.einsum('vwst,vatc->wsac', mpo_tensor[0], half_done, precisi...]
  transfers between devices with their start and end apart: 5 -> 5, of which waited for: 4 -> 5; matrix products, arithmetic and copies ran while one was open for 14% -> 3% of each run, Pallas kernels for 0% -> 5%
where the time goes in v1:
time: 1050 us
  waiting for transfers between devices  653 us (62%)
  blocking collectives  189 us (18%)
  Pallas kernels  109 us (10%)
  matrix products  47.3 us (5%)
  local copies, waits for them, and re-layouts  26.1 us (2%)
  between operations  14.1 us (1%)
  starting transfers between devices  12.7 us (1%)
    all_to_all x2, waiting for transfers between devices, swap(): lax.all_to_all(blocks, 'sector', split_axis=0, concat_axis=0, tiled=True)  304 us
    all_to_all x1, blocking collectives, swap(): lax.all_to_all(blocks, 'sector', split_axis=0, concat_axis=0, tiled=True)  189 us
    reduce_scatter x1, waiting for transfers between devices, local(): lax.psum_scatter(image, 'sector', scatter_dimension=0, tiled=True)  147 us
    all_gather x1, waiting for transfers between devices, local(): lax.all_gather(site_tensor[0].transpose(1, 0, 2), 'sector', axis=0)  113 us
    ppermute x1, waiting for transfers between devices, shifted(): return lax.ppermute(block, axis, route)  88.7 us
    pallas_call x1, Pallas kernels, carried_blocks(): pl.pallas_call(carried_kernel, grid=(rows // row_tile, parts), in_specs=[...  57 us
    pallas_call x2, Pallas kernels, env_chunk(): pl.pallas_call(env_kernel, grid=(bond // tile,), in_specs=specs, out_spec...  52 us
    dot_general x1, matrix products, local(): jnp.einsum('dkc,wbc->dwkb', bond_tensor[0].reshape(parts, columns, bond),...  23.8 us
  transfers between devices with their start and end apart: 5, of which 5 were waited for; matrix products, arithmetic and copies ran while one was open for 3% of the time, Pallas kernels for 5%

profile of v1, /device:TPU:0, one launch (start us, length us, event | category | flops | bytes accessed | tf_op | source)
XLA Modules:
  0.0 1050.6 jit_solution(15272090951721069079)
XLA Ops:
  7.2 0.0 all-gather.3.cloned.1.call-start
  7.2 3.8 copy.19
  11.0 0.0 all-gather.3.cloned.1.call-update
  11.0 2.5 collective-permute-start
  13.5 0.8 copy.12
  14.3 0.2 multiply_bitcast_fusion
  14.5 1.5 reshape.10.mix_ref
  16.0 88.7 %collective-permute-done = bf16[1,8,256,2048]{3,2,1,0:T(8,128)(2,1)} collective-permute-done((bf16[1,8,256,2048]{3,2,1,0:T(8,128)(2,1)}, bf16[1,8,256,2048]{3,2,1,0:T(8,128)(2,1)}, u32[]{:S(2)}, u32[]{:S(2)}) %collective-permute-start) | collective-permute-done | bytes 8388640 | tf_op jit(solution)/shard_map/ppermute | solution.py:20
  104.8 23.8 %convert_bitcast_fusion = bf16[8,8,256,256]{2,3,0,1:T(8,128)(2,1)} fusion(bf16[8,256,2048,1]{2,1,0,3:T(8,128)(2,1)} %bitcast.44, bf16[1,8,256,2048]{3,2,1,0:T(8,128)(2,1)} %collective-permute-done), kind=kOutput, calls=%fused_computation.5 | convolution fusion | flops 17184063488 | bytes 25165824 | tf_op jit(solution)/shard_map/dkc,wbc->dwkb/dot_general | solution.py:134
  128.5 112.6 %all-gather.3.cloned.1.call-done = bf16[16,256,2048]{2,1,0:T(8,128)(2,1)} async-done(((bf16[2,256,2048]{2,1,0:T(8,128)(2,1)}), bf16[16,256,2048]{2,1,0:T(8,128)(2,1)}) %all-gather.3.cloned.1.call-update) | async-done | bytes 16777232 | tf_op jit(solution)/shard_map/all_gather | solution.py:132
  241.2 57.0 %shard_map.68 = (bf16[8,4,2,256,256]{4,3,2,1,0:T(8,128)(2,1)}, bf16[8,4,2,256,256]{4,3,2,1,0:T(8,128)(2,1)}) custom-call(f32[256,256]{1,0:T(8,128)} %reshape.10.mix_ref, bf16[8,256,2048]{2,1,0:T(8,128)(2,1)} %bitcast.45, bf16[8,2,256,2048]{3,2,1,0:T(8,128)(2,1)} %bitcast.41), custom_call_target="tpu_custom_call" | custom-call | flops 34359738368 | bytes 100663296 | tf_op jit(solution)/shard_map/pallas_call | solution.py:63
  298.2 188.7 %all_to_all.15.x_ref = bf16[8,4,2,256,256]{4,3,2,1,0:T(8,128)(2,1)} all-to-all(bf16[8,4,2,256,256]{4,3,2,1,0:T(8,128)(2,1)} %get-tuple-element.7), channel_id=1, replica_groups=mesh['region'=4,'sector'=8] {'sector'}, dimensions={0} | all-to-all | bytes 16777216 | tf_op jit(solution)/shard_map/all_to_all | solution.py:24
  487.0 4.9 all-to-all-start.1
  491.9 7.6 copy.14
  499.5 174.6 %all-to-all-done.1.x_ref = bf16[8,4,2,256,256]{4,3,2,1,0:T(8,128)(2,1)} async-done(((bf16[8,4,2,256,256]{4,3,2,1,0:T(8,128)(2,1)}), bf16[8,4,2,256,256]{4,3,2,1,0:T(8,128)(2,1)}, u32[]{:S(2)}, u32[]{:S(2)}) %all-to-all-start.1) | async-done | bytes 8388640 | tf_op jit(solution)/shard_map/all_to_all | solution.py:24
  674.1 5.0 all-to-all-start.2
  679.1 0.2 reduce-scatter.2.cloned.1.call-start
  679.3 26.0 %shard_map.69.rest_0_ = bf16[8,256,2048]{2,1,0:T(8,128)(2,1)} custom-call(bf16[8,4,2,256,256]{4,3,2,1,0:T(8,128)(2,1)} %all-to-all-done.1.x_ref, bf16[8,2,256,2048]{3,2,1,0:T(8,128)(2,1)} %bitcast.42), custom_call_target="tpu_custom_call" | custom-call | flops 17179869184 | bytes 33554432 | tf_op jit(solution)/shard_map/pallas_call | solution.py:111
  705.3 26.0 %shard_map.70 = bf16[8,256,2048]{2,1,0:T(8,128)(2,1)} custom-call(bf16[8,4,2,256,256]{4,3,2,1,0:T(8,128)(2,1)} %all_to_all.15.x_ref, bf16[8,2,256,2048]{3,2,1,0:T(8,128)(2,1)} %bitcast.43, bf16[8,256,2048]{2,1,0:T(8,128)(2,1)} %shard_map.69.rest_0_), custom_call_target="tpu_custom_call", output_to_operand_aliasing={{}: (2, {})} | custom-call | flops 17179869184 | bytes 33554432 | tf_op jit(solution)/shard_map/pallas_call | solution.py:111
  731.3 129.7 %all-to-all-done.2 = bf16[8,8,256,256]{2,3,1,0:T(8,128)(2,1)} async-done(((bf16[8,8,256,256]{2,3,1,0:T(8,128)(2,1)}), bf16[8,8,256,256]{2,3,1,0:T(8,128)(2,1)}, u32[]{:S(2)}, u32[]{:S(2)}) %all-to-all-start.2) | async-done | bytes 8388640 | tf_op jit(solution)/shard_map/all_to_all | solution.py:24
  861.0 23.5 %bitcast_convert_fusion = bf16[2048,8,256]{0,2,1:T(8,128)(2,1)} fusion(bf16[8,8,256,256]{2,3,1,0:T(8,128)(2,1)} %all-to-all-done.2, bf16[8,256,2048]{2,1,0:T(8,128)(2,1)} %shard_map.70), kind=kOutput, calls=%fused_computation | convolution fusion | flops 17184063488 | bytes 25165824 | tf_op jit(solution)/shard_map/wka,nwkb->anb/dot_general | solution.py:149
  884.6 12.4 %copy.15 = bf16[2048,2048]{1,0:T(8,128)(2,1)} copy(bf16[2048,2048]{0,1:T(8,128)(2,1)} %bitcast.38) | data formatting | bytes 16777216 | tf_op jit(solution)/shard_map/reshape | solution.py:151
  896.9 0.0 reduce-scatter.2.cloned.1.call-update
  897.0 146.8 %reduce-scatter.2.cloned.1.call-done = bf16[256,2048]{1,0:T(8,128)(2,1)} async-done(((bf16[2048,2048]{1,0:T(8,128)(2,1)}), bf16[256,2048]{1,0:T(8,128)(2,1)}) %reduce-scatter.2.cloned.1.call-update) | async-done | bytes 1048592 | tf_op jit(solution)/shard_map/reduce_scatter | solution.py:152
  (1 shorter events, 0.0 us)
Async XLA Ops:
  7.2 234.0 %all-gather.3.cloned.1.call-start = ((), (), s32[]{:S(2)}) async-start(), calls=%async_computation.5 | async-start | bytes 18874368 | tf_op jit(solution)/shard_map/all_gather | solution.py:132
  11.0 93.7 %collective-permute-start = (bf16[1,8,256,2048]{3,2,1,0:T(8,128)(2,1)}, bf16[1,8,256,2048]{3,2,1,0:T(8,128)(2,1)}, u32[]{:S(2)}, u32[]{:S(2)}) collective-permute-start(bf16[1,8,256,2048]{3,2,1,0:T(8,128)(2,1)} %param.8), channel_id=1, source_target_pairs={{8,0},{16,8},{24,16},{0,24},{9,1},{17,9},{25,17},{1,25},{10,2},{18... | collective-permute-start | bytes 25165832 | tf_op jit(solution)/shard_map/ppermute | solution.py:20
  487.0 187.1 %all-to-all-start.1 = ((bf16[8,4,2,256,256]{4,3,2,1,0:T(8,128)(2,1)}), bf16[8,4,2,256,256]{4,3,2,1,0:T(8,128)(2,1)}, u32[]{:S(2)}, u32[]{:S(2)}) async-start(bf16[8,4,2,256,256]{4,3,2,1,0:T(8,128)(2,1)} %get-tuple-element.8), calls=%async_computation.1 | async-start | bytes 16777216 | tf_op jit(solution)/shard_map/all_to_all | solution.py:24
  674.1 187.0 %all-to-all-start.2 = ((bf16[8,8,256,256]{2,3,1,0:T(8,128)(2,1)}), bf16[8,8,256,256]{2,3,1,0:T(8,128)(2,1)}, u32[]{:S(2)}, u32[]{:S(2)}) async-start(bf16[8,8,256,256]{2,3,1,0:T(8,128)(2,1)} %copy.14), calls=%async_computation.2 | async-start | bytes 16777216 | tf_op jit(solution)/shard_map/all_to_all | solution.py:24
  679.1 364.7 %reduce-scatter.2.cloned.1.call-start = ((), (), s32[]{:S(2)}) async-start(), calls=%async_computation.4 | async-start | bytes 9437184 | tf_op jit(solution)/shard_map/reduce_scatter | solution.py:152
Sparse Core Ops, SparseCore 0:
  11.1 229.9 all-gather.2
  897.1 146.6 reduce-scatter.1

commit v2 on v1

--- a/solution.py
+++ b/solution.py
@@ -129,16 +129,21 @@
     parts = lax.axis_size("sector")
     width, rows, bond = env_left.shape[1:]
     columns = bond // parts
+    half = rows // CHUNKS
     gathered = lax.all_gather(site_tensor[0].transpose(1, 0, 2), "sector", axis=0)
     right_next = shifted(env_right, "region", -1)[0]
-    bond_blocks = jnp.einsum(
-        "dkc,wbc->dwkb",
-        bond_tensor[0].reshape(parts, columns, bond),
-        right_next,
-        preferred_element_type=jnp.float32,
-    ).astype(jnp.bfloat16)
-    bond_blocks, gathered = lax.optimization_barrier((bond_blocks, gathered))
-    bond_moved = swap(bond_blocks)
+    bond_blocks = []
+    for i in range(CHUNKS):
+        blocks = jnp.einsum(
+            "dkc,wbc->dwkb",
+            bond_tensor[0].reshape(parts, columns, bond),
+            right_next[:, i * half : (i + 1) * half],
+            preferred_element_type=jnp.float32,
+        )
+        bond_blocks.append(blocks.astype(jnp.bfloat16))
+    bond_moved = []
+    for i in range(CHUNKS):
+        bond_moved.append(swap(bond_blocks[i]))
     carried = carried_blocks(env_left[0], gathered, mpo_tensor[0], min(rows, LANES))
     moved = []
     for i in range(CHUNKS):
@@ -146,10 +151,18 @@
     env_new = None
     for i in range(CHUNKS):
         env_new = env_chunk(moved[i], gathered, env_new, i, width, 2 * LANES)
-    image = jnp.einsum(
-        "wka,nwkb->anb", env_new, bond_moved, preferred_element_type=jnp.float32
-    ).astype(jnp.bfloat16).reshape(bond, bond)
-    image_rows = lax.psum_scatter(image, "sector", scatter_dimension=0, tiled=True)
+    image_rows = []
+    for i in range(CHUNKS):
+        image = jnp.einsum(
+            "wkda,nwkb->dnba",
+            env_new.reshape(width, columns, parts, columns),
+            bond_moved[i],
+            preferred_element_type=jnp.float32,
+        ).astype(jnp.bfloat16).reshape(parts, parts * half, columns)
+        image_rows.append(lax.psum_scatter(image, "sector", scatter_dimension=0, tiled=False))
+    image_rows = jnp.stack(
+        [x.reshape(parts, half, columns) for x in image_rows], axis=1
+    ).reshape(bond, columns).T
     return (env_new[None], image_rows[None])
 
 

time: 1050 us -> 1040 us (level)
  waiting for transfers between devices: 653 us -> 640 us
    all_gather x1, waiting for transfers between devices: 113 us -> 228 us  [local(): lax.all_gather(site_tensor[0].transpose(1, 0, 2), 'sector', axis=0)]
    all_to_all x2 -> x3, waiting for transfers between devices: 304 us -> 212 us  [swap(): lax.all_to_all(blocks, 'sector', split_axis=0, concat_axis=0, tiled=True)]
    reduce_scatter x1 -> x2, waiting for transfers between devices: 147 us -> 109 us  [local(): lax.psum_scatter(image, 'sector', scatter_dimension=0, tiled=False)]
    reshape x1 -> x0, local copies, waits for them, and re-layouts: 12.4 us -> none  [local(): image = jnp.einsum('wka,nwkb->anb', env_new, bond_moved, preferred_elemen...]
    dot_general x1 -> x2, matrix products: 23.8 us -> 26.5 us  [local(): jnp.einsum('dkc,wbc->dwkb', bond_tensor[0].reshape(parts, columns, bond),...]
    dot_general x1 -> x2, matrix products: 23.5 us -> 25 us  [local(): jnp.einsum('wkda,nwkb->dnba', env_new.reshape(width, columns, parts, colu...]
  transfers between devices with their start and end apart: 5 -> 7, of which waited for: 5 -> 7; matrix products, arithmetic and copies ran while one was open for 3% -> 6% of each run, Pallas kernels for 5% -> 5%
where the time goes in v2:
time: 1040 us
  waiting for transfers between devices  640 us (62%)
  blocking collectives  189 us (18%)
  Pallas kernels  109 us (10%)
  matrix products  51.5 us (5%)
  local copies, waits for them, and re-layouts  15.9 us (2%)
  starting transfers between devices  14.6 us (1%)
  between operations  13.8 us (1%)
    all_gather x1, waiting for transfers between devices, local(): lax.all_gather(site_tensor[0].transpose(1, 0, 2), 'sector', axis=0)  228 us
    all_to_all x3, waiting for transfers between devices, swap(): lax.all_to_all(blocks, 'sector', split_axis=0, concat_axis=0, tiled=True)  212 us
    all_to_all x1, blocking collectives, swap(): lax.all_to_all(blocks, 'sector', split_axis=0, concat_axis=0, tiled=True)  189 us
    reduce_scatter x2, waiting for transfers between devices, local(): lax.psum_scatter(image, 'sector', scatter_dimension=0, tiled=False)  109 us
    ppermute x1, waiting for transfers between devices, shifted(): return lax.ppermute(block, axis, route)  91.3 us
    pallas_call x1, Pallas kernels, carried_blocks(): pl.pallas_call(carried_kernel, grid=(rows // row_tile, parts), in_specs=[...  57 us
    pallas_call x2, Pallas kernels, env_chunk(): pl.pallas_call(env_kernel, grid=(bond // tile,), in_specs=specs, out_spec...  52 us
    dot_general x2, matrix products, local(): jnp.einsum('dkc,wbc->dwkb', bond_tensor[0].reshape(parts, columns, bond),...  26.5 us
  transfers between devices with their start and end apart: 7, of which 7 were waited for; matrix products, arithmetic and copies ran while one was open for 6% of the time, Pallas kernels for 5%

profile of v2, /device:TPU:0, one launch (start us, length us, event | category | flops | bytes accessed | tf_op | source)
XLA Modules:
  0.0 1035.5 jit_solution(13894182775853802563)
XLA Ops:
  7.2 0.0 all-gather.3.cloned.1.call-start
  7.2 3.8 copy.53
  11.0 0.0 all-gather.3.cloned.1.call-update
  11.0 0.8 copy.26
  11.8 0.2 multiply_bitcast_fusion
  12.0 1.5 reshape.20.mix_ref
  13.6 227.6 %all-gather.3.cloned.1.call-done = bf16[16,256,2048]{2,1,0:T(8,128)(2,1)} async-done(((bf16[2,256,2048]{2,1,0:T(8,128)(2,1)}), bf16[16,256,2048]{2,1,0:T(8,128)(2,1)}) %all-gather.3.cloned.1.call-update) | async-done | bytes 16777232 | tf_op jit(solution)/shard_map/all_gather | solution.py:133
  241.2 57.0 %shard_map.68 = (bf16[8,4,2,256,256]{4,3,2,1,0:T(8,128)(2,1)}, bf16[8,4,2,256,256]{4,3,2,1,0:T(8,128)(2,1)}) custom-call(f32[256,256]{1,0:T(8,128)} %reshape.20.mix_ref, bf16[8,256,2048]{2,1,0:T(8,128)(2,1)} %bitcast.100, bf16[8,2,256,2048]{3,2,1,0:T(8,128)(2,1)} %bitcast.97), custom_call_target="tpu_custom_call" | custom-call | flops 34359738368 | bytes 100663296 | tf_op jit(solution)/shard_map/pallas_call | solution.py:63
  298.2 188.8 %all_to_all.20.x_ref = bf16[8,4,2,256,256]{4,3,2,1,0:T(8,128)(2,1)} all-to-all(bf16[8,4,2,256,256]{4,3,2,1,0:T(8,128)(2,1)} %get-tuple-element.5), channel_id=1, replica_groups=mesh['region'=4,'sector'=8] {'sector'}, dimensions={0} | all-to-all | bytes 16777216 | tf_op jit(solution)/shard_map/all_to_all | solution.py:24
  487.0 5.0 all-to-all-start
  491.9 0.1 collective-permute-start
  492.0 91.3 %collective-permute-done = bf16[1,8,256,2048]{3,2,1,0:T(8,128)(2,1)S(1)} collective-permute-done((bf16[1,8,256,2048]{3,2,1,0:T(8,128)(2,1)}, bf16[1,8,256,2048]{3,2,1,0:T(8,128)(2,1)S(1)}, u32[]{:S(2)}, u32[]{:S(2)}) %collective-permute-start) | collective-permute-done | bytes 8388640 | tf_op jit(solution)/shard_map/ppermute | solution.py:20
  583.3 0.0 copy-start
  583.3 3.4 copy-done
  586.7 12.6 %convert_bitcast_fusion.1 = bf16[8,8,256,128]{2,3,1,0:T(8,128)(2,1)} fusion(bf16[8,256,2048,1]{2,1,3,0:T(8,128)(2,1)} %bitcast.101, bf16[8,256,2048]{2,1,0:T(8,128)(2,1)S(1)} %bitcast.103), kind=kOutput, calls=%fused_computation.16 | convolution fusion | flops 8592031744 | bytes 16777216 | tf_op jit(solution)/shard_map/dkc,wbc->dwkb/dot_general | solution.py:137
  599.2 74.9 %all-to-all-done.x_ref = bf16[8,4,2,256,256]{4,3,2,1,0:T(8,128)(2,1)} async-done(((bf16[8,4,2,256,256]{4,3,2,1,0:T(8,128)(2,1)}), bf16[8,4,2,256,256]{4,3,2,1,0:T(8,128)(2,1)}, u32[]{:S(2)}, u32[]{:S(2)}) %all-to-all-start) | async-done | bytes 8388640 | tf_op jit(solution)/shard_map/all_to_all | solution.py:24
  674.1 4.7 all-to-all-start.2
  678.8 14.0 %convert_bitcast_fusion = bf16[8,8,256,128]{2,3,1,0:T(8,128)(2,1)} fusion(bf16[8,256,2048,1]{2,1,3,0:T(8,128)(2,1)} %bitcast.102, bf16[8,256,2048]{2,1,0:T(8,128)(2,1)} %bitcast.104), kind=kOutput, calls=%fused_computation.15 | convolution fusion | flops 8592031744 | bytes 16777216 | tf_op jit(solution)/shard_map/dkc,wbc->dwkb/dot_general | solution.py:137
  692.8 26.0 %shard_map.69.rest_0_ = bf16[8,256,2048]{2,1,0:T(8,128)(2,1)} custom-call(bf16[8,4,2,256,256]{4,3,2,1,0:T(8,128)(2,1)} %all_to_all.20.x_ref, bf16[8,2,256,2048]{3,2,1,0:T(8,128)(2,1)} %bitcast.98), custom_call_target="tpu_custom_call" | custom-call | flops 17179869184 | bytes 33554432 | tf_op jit(solution)/shard_map/pallas_call | solution.py:111
  718.8 26.0 %shard_map.70 = bf16[8,256,2048]{2,1,0:T(8,128)(2,1)} custom-call(bf16[8,4,2,256,256]{4,3,2,1,0:T(8,128)(2,1)} %all-to-all-done.x_ref, bf16[8,2,256,2048]{3,2,1,0:T(8,128)(2,1)} %bitcast.99, bf16[8,256,2048]{2,1,0:T(8,128)(2,1)} %shard_map.69.rest_0_), custom_call_target="tpu_custom_call", output_to_operand_aliasing={{}: (2, {})} | custom-call | flops 17179869184 | bytes 33554432 | tf_op jit(solution)/shard_map/pallas_call | solution.py:111
  744.8 26.5 %all-to-all-done.2 = bf16[8,8,256,128]{2,3,1,0:T(8,128)(2,1)} async-done(((bf16[8,8,256,128]{2,3,1,0:T(8,128)(2,1)}), bf16[8,8,256,128]{2,3,1,0:T(8,128)(2,1)}, u32[]{:S(2)}, u32[]{:S(2)}) %all-to-all-start.2) | async-done | bytes 4194336 | tf_op jit(solution)/shard_map/all_to_all | solution.py:24
  771.3 4.6 all-to-all-start.3
  775.8 0.3 reduce-scatter.3.cloned.1.call-start
  776.1 12.5 %fusion.4 = bf16[8,8,128,256]{3,2,0,1:T(8,128)(2,1)S(1)} fusion(bf16[8,32,8,8,256]{4,3,2,1,0:T(8,128)(2,1)} %bitcast.105, bf16[8,8,256,128]{2,3,1,0:T(8,128)(2,1)} %all-to-all-done.2), kind=kOutput, calls=%fused_computation.7 | convolution fusion | flops 8592031744 | bytes 16777216 | tf_op jit(solution)/shard_map/wkda,nwkb->dnba/dot_general | solution.py:156
  788.6 2.4 copy.29
  791.1 0.0 reduce-scatter.3.cloned.1.call-update
  791.1 0.0 reduce-scatter.5.cloned.1.call-start
  791.1 110.8 %all-to-all-done.3 = bf16[8,8,256,128]{2,3,1,0:T(8,128)(2,1)} async-done(((bf16[8,8,256,128]{2,3,1,0:T(8,128)(2,1)}), bf16[8,8,256,128]{2,3,1,0:T(8,128)(2,1)}, u32[]{:S(2)}, u32[]{:S(2)}) %all-to-all-start.3) | async-done | bytes 4194336 | tf_op jit(solution)/shard_map/all_to_all | solution.py:24
  901.9 12.5 %fusion.5 = bf16[8,8,128,256]{3,2,0,1:T(8,128)(2,1)S(1)} fusion(bf16[8,32,8,8,256]{4,3,2,1,0:T(8,128)(2,1)} %bitcast.106, bf16[8,8,256,128]{2,3,1,0:T(8,128)(2,1)} %all-to-all-done.3), kind=kOutput, calls=%fused_computation.8 | convolution fusion | flops 8592031744 | bytes 16777216 | tf_op jit(solution)/shard_map/wkda,nwkb->dnba/dot_general | solution.py:156
  914.4 2.5 copy.31
  916.9 0.0 reduce-scatter.5.cloned.1.call-update
  916.9 17.7 %reduce-scatter.3.cloned.1.call-done = bf16[1,1024,256]{2,1,0:T(8,128)(2,1)} async-done(((bf16[8,1024,256]{2,1,0:T(8,128)(2,1)}), bf16[1,1024,256]{2,1,0:T(8,128)(2,1)}) %reduce-scatter.3.cloned.1.call-update) | async-done | bytes 524304 | tf_op jit(solution)/shard_map/reduce_scatter | solution.py:162
  934.6 91.6 %reduce-scatter.5.cloned.1.call-done = bf16[1,1024,256]{2,1,0:T(8,128)(2,1)} async-done(((bf16[8,1024,256]{2,1,0:T(8,128)(2,1)}), bf16[1,1024,256]{2,1,0:T(8,128)(2,1)}) %reduce-scatter.5.cloned.1.call-update) | async-done | bytes 524304 | tf_op jit(solution)/shard_map/reduce_scatter | solution.py:162
  1026.2 1.3 pad_maximum_fusion
  1027.5 0.1 copy.32
  1027.6 1.4 copy.33
  (1 shorter events, 0.0 us)
Async XLA Ops:
  7.2 234.0 %all-gather.3.cloned.1.call-start = ((), (), s32[]{:S(2)}) async-start(), calls=%async_computation.8 | async-start | bytes 18874368 | tf_op jit(solution)/shard_map/all_gather | solution.py:133
  487.0 187.1 %all-to-all-start = ((bf16[8,4,2,256,256]{4,3,2,1,0:T(8,128)(2,1)}), bf16[8,4,2,256,256]{4,3,2,1,0:T(8,128)(2,1)}, u32[]{:S(2)}, u32[]{:S(2)}) async-start(bf16[8,4,2,256,256]{4,3,2,1,0:T(8,128)(2,1)} %get-tuple-element.4), calls=%async_computation | async-start | bytes 16777216 | tf_op jit(solution)/shard_map/all_to_all | solution.py:24
  491.9 91.3 %collective-permute-start = (bf16[1,8,256,2048]{3,2,1,0:T(8,128)(2,1)}, bf16[1,8,256,2048]{3,2,1,0:T(8,128)(2,1)S(1)}, u32[]{:S(2)}, u32[]{:S(2)}) collective-permute-start(bf16[1,8,256,2048]{3,2,1,0:T(8,128)(2,1)} %param.8), channel_id=1, source_target_pairs={{8,0},{16,8},{24,16},{0,24},{9,1},{17,9},{25,17},{1,25},{10,2},{18... | collective-permute-start | bytes 25165832 | tf_op jit(solution)/shard_map/ppermute | solution.py:20
  583.3 3.4 copy-start
  674.1 97.2 %all-to-all-start.2 = ((bf16[8,8,256,128]{2,3,1,0:T(8,128)(2,1)}), bf16[8,8,256,128]{2,3,1,0:T(8,128)(2,1)}, u32[]{:S(2)}, u32[]{:S(2)}) async-start(bf16[8,8,256,128]{2,3,1,0:T(8,128)(2,1)} %convert_bitcast_fusion.1), calls=%async_computation.2 | async-start | bytes 8388608 | tf_op jit(solution)/shard_map/all_to_all | solution.py:24
  771.3 130.7 %all-to-all-start.3 = ((bf16[8,8,256,128]{2,3,1,0:T(8,128)(2,1)}), bf16[8,8,256,128]{2,3,1,0:T(8,128)(2,1)}, u32[]{:S(2)}, u32[]{:S(2)}) async-start(bf16[8,8,256,128]{2,3,1,0:T(8,128)(2,1)} %convert_bitcast_fusion), calls=%async_computation.4 | async-start | bytes 8388608 | tf_op jit(solution)/shard_map/all_to_all | solution.py:24
  775.8 158.8 %reduce-scatter.3.cloned.1.call-start = ((), (), s32[]{:S(2)}) async-start(), calls=%async_computation.6 | async-start | bytes 4718592 | tf_op jit(solution)/shard_map/reduce_scatter | solution.py:162
  791.1 235.1 %reduce-scatter.5.cloned.1.call-start = ((), (), s32[]{:S(2)}) async-start(), calls=%async_computation.7 | async-start | bytes 4718592 | tf_op jit(solution)/shard_map/reduce_scatter | solution.py:162
Sparse Core Ops, SparseCore 0:
  11.1 229.9 all-gather.2
  791.2 143.3 reduce-scatter.2
  938.3 87.8 reduce-scatter.4
